TPU v7x, 256 devices: a whole 4x4x8 slice. The times are simulated.
256 devices in a mesh: grp: 2 (over core), fsdp: 16 (over y, z_lo), tp: 8 (over x, z_hi).
Axes of the slice: x: 4, y: 4, z: 8 (z_hi: 2, z_lo: 4; z = z_hi * 4 + z_lo), core: 2. Of those that a mesh axis runs over, the one named last changes fastest.
Arguments:
- frames: bfloat16 [2, 4096, 8192], P('grp', 'fsdp'), may hold values from -6 to 6
- rewards: bfloat16 [4096], P('fsdp'), may hold values from -5 to 5
- actions: int32 [2, 4096], P('grp', 'fsdp'), may hold values from 0 to 17
- fractions: int32 [2, 4096, 32], P('grp', 'fsdp'), may hold values from 0 to 63
- episode_shard: int32 [4096, 1], P('fsdp'), may hold values from 0 to 15, as said below
- table: float32 [64], replicated, may hold values from 0.02 to 0.98
- norm_gain: float32 [8192], replicated, may hold values from 0.1 to 1.9
- torso_weight: bfloat16 [8192, 4096], P(('grp', 'fsdp'), 'tp'), may hold values from -0.0625 to 0.0625
- embed_weight: bfloat16 [64, 4096], P(None, 'tp'), may hold values from -0.75 to 0.75
- value_weight: bfloat16 [18, 4096], P(None, 'tp'), may hold values from -0.59765625 to 0.59765625
Outputs:
- torso_grad: float32 [8192, 4096], P(('grp', 'fsdp'), 'tp')
- refreshed_weight: bfloat16 [8192, 4096], P(('grp', 'fsdp', 'tp'))
Inputs may be any that keep to these rules, and one draw needn't show every extreme that they name: `episode_shard`: of the rows of one index of fsdp, at most 24 belong to one learner shard, and in every such block some learner shard gets exactly 24; every learner shard gets at least one row from every block.
All inputs are finite; a program needn't handle non-finite values.
Results may differ from a plain program's by a relative error of at most 0.0075.
Values may be sent and summed in bfloat16 or wider, within the bound.
No kernel may reach another device: no remote copies, remote signals or barrier semaphores. Data moves between devices by JAX's collectives and lax.ppermute only.
A program may use at most 64 MiB of HBM per device.

v0:
```python
import jax
import jax.numpy as jnp
from jax import lax
from jax.sharding import PartitionSpec as P

ACTIONS = 18
COSINES = 64
FRACS = 64
Z = 4
Y = 4
SWAP = [(0, 1), (1, 0)]


def z_from(step):
    return [(f, f // Z * Z + (f % Z - step) % Z) for f in range(Y * Z)]


def y_from(step):
    return [(f, (f - step * Z) % (Y * Z)) for f in range(Y * Z)]


def roll_from(array, start, axis):
    size = array.shape[axis]
    return lax.dynamic_slice_in_dim(jnp.concatenate([array, array], axis), start, size, axis)


def shards(
    frames,
    rewards,
    actions,
    fractions,
    episode_shard,
    table,
    norm_gain,
    torso_weight,
    embed_weight,
    value_weight,
):
    group = lax.axis_index("grp")
    place = lax.axis_index("fsdp")
    shard_total = lax.axis_size("fsdp")
    whole = lax.all_gather(torso_weight, ("grp", "fsdp"), axis=0, tiled=True)
    rows_block = frames.shape[1]
    width = frames.shape[2]
    half = rows_block // 2
    own_rows = group * half
    other_rows = (1 - group) * half

    def swap(array):
        kept = lax.dynamic_slice_in_dim(array, own_rows, half, 0)
        sent = lax.dynamic_slice_in_dim(array, other_rows, half, 0)
        got = lax.ppermute(sent, "grp", SWAP)
        return (jnp.where(group == 0, kept, got), jnp.where(group == 0, got, kept))

    with jax.named_scope("rows_swap"):
        target_rows, online_rows = swap(frames[0])
        ints = jnp.concatenate([fractions[0].T, actions[0][None, :]], 0)
        target_ints, online_ints = swap(ints.T)
        ints_all = jnp.concatenate([target_ints, online_ints], 0).T
        fraction_rows = ints_all[:-1]
        action_rows = ints_all[-1]

    def norm(rows):
        values = rows.astype(jnp.float32)
        mean_square = jnp.mean(values * values, axis=-1, keepdims=True)
        return (values * lax.rsqrt(mean_square + 1e-05) * norm_gain).astype(jnp.bfloat16)

    normed_target = norm(target_rows)
    normed_online = norm(online_rows)
    normed = jnp.concatenate([normed_target, normed_online], 0)
    with jax.named_scope("columns_exchange"):
        block = width // (2 * shard_total)
        own_cols = lax.dynamic_slice_in_dim(normed_online, group * (width // 2), width // 2, 1)
        other_cols = lax.dynamic_slice_in_dim(
            normed_online, (1 - group) * (width // 2), width // 2, 1
        )
        pieces = jnp.stack(
            [
                own_cols.reshape(half, shard_total, block),
                other_cols.reshape(half, shard_total, block),
            ],
            2,
        )
        pieces = jnp.transpose(pieces, (1, 0, 2, 3)).reshape(shard_total, half, 2 * block)
        columns = lax.all_to_all(pieces, "fsdp", 0, 0, tiled=True)
        columns = columns.reshape(Y, Z, half, 2 * block)
        columns = roll_from(roll_from(columns, place // Z, 0), place % Z, 1)
    with jax.named_scope("counts"):
        lanes = jnp.arange(shard_total, dtype=jnp.int32)
        onehot = episode_shard[:, :1] == lanes[None, :]
        local_counts = jnp.sum(onehot.astype(jnp.float32), axis=0)
        counts = jnp.sum(
            lax.all_to_all(
                jnp.broadcast_to(local_counts[None, :], (shard_total, shard_total)),
                "fsdp",
                0,
                0,
                tiled=True,
            ),
            axis=0,
        )
        inverse = float(rows_block) / counts
        row_weight = jnp.sum(jnp.where(onehot, inverse[None, :], 0.0), axis=1)
        row_weight = lax.dynamic_slice_in_dim(row_weight, own_rows, half, 0)
    choose_mask = (action_rows[:, None] == jnp.arange(ACTIONS, dtype=jnp.int32)[None, :]).astype(
        jnp.bfloat16
    )
    picked = jnp.dot(choose_mask, value_weight, preferred_element_type=jnp.float32)
    cosine = jnp.cos(
        jnp.pi * jnp.arange(COSINES, dtype=jnp.float32)[None, :] * table[:, None]
    ).astype(jnp.bfloat16)
    embedding = jax.nn.relu(
        jnp.dot(cosine, embed_weight, preferred_element_type=jnp.float32)
    ).astype(jnp.bfloat16)
    ids = jnp.arange(FRACS, dtype=jnp.int32)
    online_fractions = fraction_rows[:, half:]
    online_select = online_fractions[:, None, :] == ids[None, :, None]
    levels = jnp.sum(jnp.where(online_select, table[None, :, None], 0.0), axis=1)
    reward_rows = lax.dynamic_slice_in_dim(rewards, own_rows, half, 0).astype(jnp.float32)
    preact = jnp.dot(normed, whole, preferred_element_type=jnp.float32)
    weighted = (jax.nn.silu(preact) * picked).astype(jnp.bfloat16)
    table_values = lax.dot_general(
        embedding, weighted, (((1,), (1,)), ((), ())), preferred_element_type=jnp.float32
    )
    partial_quant = jnp.sum(
        jnp.where(fraction_rows[:, None, :] == ids[None, :, None], table_values[None, :, :], 0.0),
        axis=1,
    )
    with jax.named_scope("quant_sum"):
        tp_total = lax.axis_size("tp")
        quant = jnp.sum(
            lax.all_to_all(
                jnp.broadcast_to(partial_quant[None], (tp_total,) + partial_quant.shape),
                "tp",
                0,
                0,
                tiled=True,
            ),
            axis=0,
        )
    target_quant = quant[:, :half]
    online_quant = quant[:, half:]
    target_value = reward_rows[None, :] + 0.99 * target_quant
    errors = target_value[None, :, :] - online_quant[:, None, :]
    weight = jnp.abs(levels[:, None, :] - (errors < 0).astype(jnp.float32))
    grad_quant = -row_weight[None, :] * jnp.sum(weight * jnp.clip(errors, -1.0, 1.0), axis=1)
    grad_table = jnp.sum(jnp.where(online_select, grad_quant[:, None, :], 0.0), axis=0)
    grad_feature = lax.dot_general(
        grad_table,
        embedding.astype(jnp.float32),
        (((0,), (0,)), ((), ())),
        precision=lax.Precision.HIGHEST,
    )
    online_preact = preact[half:]
    gate_value = jax.nn.sigmoid(online_preact)
    grad_preact = (
        grad_feature * picked[half:] * gate_value * (1.0 + online_preact * (1.0 - gate_value))
    ).astype(jnp.bfloat16)
    with jax.named_scope("grad_gather"):
        quad = jnp.stack(
            [grad_preact] + [lax.ppermute(grad_preact, "fsdp", z_from(k)) for k in range(1, Z)]
        )
        below = lax.ppermute(quad, "fsdp", y_from(1))
        above = lax.ppermute(quad, "fsdp", y_from(3))
        far_low = lax.ppermute(above[: Z // 2], "fsdp", y_from(3))
        far_high = lax.ppermute(below[Z // 2 :], "fsdp", y_from(1))

    def product(cols, grads):
        return lax.dot_general(
            cols.reshape(-1, cols.shape[-1]),
            grads.reshape(-1, grads.shape[-1]),
            (((0,), (0,)), ((), ())),
            preferred_element_type=jnp.float32,
        )

    part = (
        product(columns[0], quad)
        + product(columns[1], below)
        + product(columns[3], above)
        + product(columns[2, : Z // 2], far_low)
        + product(columns[2, Z // 2 :], far_high)
    )
    torso_grad = part[:block] + lax.ppermute(part[block:], "grp", SWAP)
    updated = (torso_weight.astype(jnp.float32) - 0.01 * torso_grad).astype(jnp.bfloat16)
    refreshed_weight = lax.all_to_all(updated, "tp", split_axis=0, concat_axis=1, tiled=True)
    return (torso_grad, refreshed_weight)


def solution(mesh):
    placed = (
        P("grp", "fsdp", None),
        P("fsdp"),
        P("grp", "fsdp"),
        P("grp", "fsdp", None),
        P("fsdp", None),
        P(),
        P(),
        P(("grp", "fsdp"), "tp"),
        P(None, "tp"),
        P(None, "tp"),
    )
    return jax.shard_map(
        shards,
        mesh=mesh,
        in_specs=placed,
        out_specs=(P(("grp", "fsdp"), "tp"), P(("grp", "fsdp", "tp"), None)),
        check_vma=False,
    )
```

profile of v0, /device:TPU:1, one launch (start us, length us, event | category | flops | bytes accessed | tf_op | source)
XLA Modules:
  0.0 217.1 jit_solution(5258170492067754753)
XLA Ops:
  7.2 0.7 all-gather.2.cloned.1.call-update
  7.9 3.1 %dynamic-slice_bitcast_fusion = bf16[128,8192]{1,0:T(8,128)(2,1)} fusion(bf16[1,256,8192]{2,1,0:T(8,128)(2,1)} %param.10, s32[]{:T(128)S(6)} %select_n.74), kind=kLoop, calls=%fused_computation.25 | loop fusion | bytes 4194308 | tf_op jit(solution)/shard_map/rows_swap/dynamic_slice | solution.py:51
  11.1 3.2 %collective-permute-start = (bf16[128,8192]{1,0:T(8,128)(2,1)}, bf16[128,8192]{1,0:T(8,128)(2,1)S(1)}, u32[]{:S(2)}, u32[]{:S(2)}) collective-permute-start(bf16[128,8192]{1,0:T(8,128)(2,1)} %dynamic-slice_bitcast_fusion), channel_id=1, source_target_pairs={{0,128},{128,0},{1,129},{129,1},{2,130},{130,2},{3,131},{131,3},{4... | collective-permute-start | bytes 6291464 | tf_op jit(solution)/shard_map/rows_swap/ppermute | solution.py:52
  14.4 0.6 broadcast_in_dim.46
  15.1 6.6 %all-to-all-start.1 = ((f32[16,1,16]{2,1,0:T(1,128)}), f32[16,1,16]{2,1,0:T(1,128)S(1)}, u32[]{:S(2)}, u32[]{:S(2)}) async-start(f32[16,1,16]{2,1,0:T(1,128)} %broadcast_in_dim.46), calls=%async_computation.1 | async-start | bytes 16384 | tf_op jit(solution)/shard_map/counts/all_to_all | solution.py:93
  21.7 3.9 %fusion.3 = (f32[128]{0:T(128)S(1)}, f32[128]{0:T(128)S(1)}) fusion(bf16[128,8192]{1,0:T(8,128)(2,1)S(1)} %collective-permute-done, bf16[1,256,8192]{2,1,0:T(8,128)(2,1)} %param.10, s32[]{:T(128)S(6)} %select_n.75, pred[]{:T(512)S(6)} %eq.32), kind=kLoop, calls=%fused_computation.7 | loop fusion | flops 8388352 | bytes 4195333 | tf_op jit(solution)/shard_map/reduce_sum | solution.py:65
  25.7 4.4 %fusion.5 = (bf16[128,8192]{1,0:T(8,128)(2,1)}, bf16[128,8192]{1,0:T(8,128)(2,1)S(1)}) fusion(f32[128]{0:T(128)S(1)} %get-tuple-element.19, f32[8192]{0:T(1024)S(1)} %copy-done.5, bf16[128,8192]{1,0:T(8,128)(2,1)} %copy-done.2, bf16[1,256,8192]{2,1,0:T(8,128)(2,1)S(1)} %copy-done.1, s32[]{:T(128)S(6)} %select_n.75, pred[]{:T(512)S(6)} %eq.32, ...), kind=kLoop, calls=%fused_computation.9 | loop fusion | flops 10485760 | bytes 8422405 | tf_op jit(solution)/shard_map/convert_element_type | solution.py:66
  30.1 1.2 constant_dynamic-slice_fusion.1
  31.3 2.3 %copy.29 = bf16[128,4096]{0,1:T(8,128)(2,1)} copy(bf16[128,4096]{1,0:T(8,128)(2,1)} %get-tuple-element.13) | data formatting | bytes 2097152 | tf_op jit(solution)/shard_map/columns_exchange/dynamic_slice | solution.py:73
  33.6 1.3 copy.30
  34.9 1.8 maximum_bitcast_fusion
  36.7 1.5 copy.31
  38.2 7.1 %all-to-all-start = ((bf16[16,128,512]{1,2,0:T(8,128)(2,1)}), bf16[16,128,512]{1,2,0:T(8,128)(2,1)}, u32[]{:S(2)}, u32[]{:S(2)}) async-start(bf16[16,128,512]{1,2,0:T(8,128)(2,1)} %bitcast.69), calls=%async_computation | async-start | bytes 4194304 | tf_op jit(solution)/shard_map/columns_exchange/all_to_all | solution.py:85
  45.3 0.9 collective-permute-start.1
  46.2 0.3 fusion.17
  46.6 0.4 collective-permute-done.1
  47.4 75.1 %all-gather.2.cloned.1.call-done = bf16[8192,512]{1,0:T(8,128)(2,1)} async-done(((bf16[256,512]{1,0:T(8,128)(2,1)}), bf16[8192,512]{1,0:T(8,128)(2,1)}) %all-gather.2.cloned.1.call-update) | async-done | bytes 8388624 | tf_op jit(solution)/shard_map/all_gather | solution.py:42
  122.5 6.3 %fusion.6 = f32[256,512]{1,0:T(8,128)S(1)} fusion(bf16[8192,512]{1,0:T(8,128)(2,1)} %all-gather.2.cloned.1.call-done, bf16[128,8192]{1,0:T(8,128)(2,1)S(1)} %get-tuple-element.7, bf16[128,8192]{1,0:T(8,128)(2,1)} %get-tuple-element.6), kind=kOutput, calls=%fused_computation.14 | convolution fusion | flops 2155872256 | bytes 13107200 | tf_op jit(solution)/shard_map/dot_general | solution.py:120
  128.8 0.8 copy-done.11
  129.6 0.3 fusion.20
  129.9 0.4 select_reduce_fusion
  130.3 0.7 broadcast_in_dim.53
  131.0 7.4 %all-to-all-start.2 = ((f32[8,32,256]{2,1,0:T(8,128)}), f32[8,32,256]{2,1,0:T(8,128)S(1)}, u32[]{:S(2)}, u32[]{:S(2)}) async-start(f32[8,32,256]{2,1,0:T(8,128)} %broadcast_in_dim.53), calls=%async_computation.2 | async-start | bytes 524288 | tf_op jit(solution)/shard_map/quant_sum/all_to_all | solution.py:132
  138.8 2.8 %copy.32 = bf16[4,4,128,512]{3,2,1,0:T(8,128)(2,1)S(1)} copy(bf16[4,4,128,512]{2,3,1,0:T(8,128)(2,1)} %bitcast.6) | data formatting | bytes 4194304 | tf_op jit(solution)/shard_map/columns_exchange/reshape | solution.py:86
  141.6 7.7 %all-to-all-done.2 = f32[8,32,256]{2,1,0:T(8,128)S(1)} async-done(((f32[8,32,256]{2,1,0:T(8,128)}), f32[8,32,256]{2,1,0:T(8,128)S(1)}, u32[]{:S(2)}, u32[]{:S(2)}) %all-to-all-start.2) | async-done | bytes 262176 | tf_op jit(solution)/shard_map/quant_sum/all_to_all | solution.py:132
  149.7 1.3 fusion.16
  151.0 1.7 collective-permute-start.2
  152.7 2.3 %collective-permute-start.3 = (bf16[128,512]{1,0:T(8,128)(2,1)S(1)}, bf16[128,512]{1,0:T(8,128)(2,1)S(1)}, u32[]{:S(2)}, u32[]{:S(2)}) collective-permute-start(bf16[128,512]{1,0:T(8,128)(2,1)S(1)} %fusion.16), channel_id=1, source_target_pairs={{0,16},{8,24},{16,0},{24,8},{32,48},{40,56},{48,32},{56,40},{64,80... | collective-permute-start | bytes 393224 | tf_op jit(solution)/shard_map/grad_gather/ppermute | solution.py:161
  155.0 1.0 collective-permute-start.4
  156.0 0.7 fusion.11
  156.8 4.7 %collective-permute-done.3 = bf16[128,512]{1,0:T(8,128)(2,1)S(1)} collective-permute-done((bf16[128,512]{1,0:T(8,128)(2,1)S(1)}, bf16[128,512]{1,0:T(8,128)(2,1)S(1)}, u32[]{:S(2)}, u32[]{:S(2)}) %collective-permute-start.3) | collective-permute-done | bytes 131104 | tf_op jit(solution)/shard_map/grad_gather/ppermute | solution.py:161
  161.4 1.5 collective-permute-done.4
  163.0 6.2 %collective-permute-start.5 = (bf16[4,128,512]{2,1,0:T(8,128)(2,1)S(1)}, bf16[4,128,512]{2,1,0:T(8,128)(2,1)S(1)}, u32[]{:S(2)}, u32[]{:S(2)}) collective-permute-start(bf16[4,128,512]{2,1,0:T(8,128)(2,1)S(1)} %pad_maximum_fusion), channel_id=1, source_target_pairs={{0,96},{8,104},{16,112},{24,120},{32,0},{40,8},{48,16},{56,24},{64... | collective-permute-start | bytes 1572872 | tf_op jit(solution)/shard_map/grad_gather/ppermute | solution.py:163
  169.2 0.5 collective-permute-start.6
  169.6 0.7 fusion.10
  170.5 11.6 %collective-permute-done.6 = bf16[4,128,512]{2,1,0:T(8,128)(2,1)S(1)} collective-permute-done((bf16[4,128,512]{2,1,0:T(8,128)(2,1)S(1)}, bf16[4,128,512]{2,1,0:T(8,128)(2,1)S(1)}, u32[]{:S(2)}, u32[]{:S(2)}) %collective-permute-start.6) | collective-permute-done | bytes 524320 | tf_op jit(solution)/shard_map/grad_gather/ppermute | solution.py:164
  182.3 2.7 %collective-permute-start.8 = (bf16[2,128,512]{2,1,0:T(8,128)(2,1)S(1)}, bf16[2,128,512]{2,1,0:T(8,128)(2,1)S(1)}, u32[]{:S(2)}, u32[]{:S(2)}) collective-permute-start(bf16[2,128,512]{2,1,0:T(8,128)(2,1)S(1)} %slice.78), channel_id=1, source_target_pairs={{0,96},{8,104},{16,112},{24,120},{32,0},{40,8},{48,16},{56,24},{64... | collective-permute-start | bytes 786440 | tf_op jit(solution)/shard_map/grad_gather/ppermute | solution.py:166
  185.1 0.5 fusion.34
  185.5 0.5 convolution_add_fusion.1
  186.0 2.7 %collective-permute-done.7 = bf16[2,128,512]{2,1,0:T(8,128)(2,1)S(1)} collective-permute-done((bf16[2,128,512]{2,1,0:T(8,128)(2,1)S(1)}, bf16[2,128,512]{2,1,0:T(8,128)(2,1)S(1)}, u32[]{:S(2)}, u32[]{:S(2)}) %collective-permute-start.7) | collective-permute-done | bytes 262176 | tf_op jit(solution)/shard_map/grad_gather/ppermute | solution.py:165
  188.7 0.3 fusion.35
  189.1 0.3 fusion.36
  189.4 0.5 fusion.13
  189.9 3.8 %collective-permute-start.9 = (f32[256,512]{1,0:T(8,128)S(1)}, f32[256,512]{1,0:T(8,128)S(1)}, u32[]{:S(2)}, u32[]{:S(2)}) collective-permute-start(f32[256,512]{1,0:T(8,128)S(1)} %slice.80), channel_id=1, source_target_pairs={{0,128},{128,0},{1,129},{129,1},{2,130},{130,2},{3,131},{131,3},{4... | collective-permute-start | bytes 1572872 | tf_op jit(solution)/shard_map/ppermute | solution.py:183
  193.7 1.5 collective-permute-done.9
  195.2 0.9 subtract_convert_fusion
  196.2 13.3 %all_to_all.35 = bf16[8,32,512]{2,1,0:T(8,128)(2,1)S(1)} all-to-all(bf16[8,32,512]{2,1,0:T(8,128)(2,1)S(1)} %bitcast.81), channel_id=1, replica_groups=mesh['grp'=2,'fsdp'=16,'tp'=8] {'tp'}, dimensions={0} | all-to-all | bytes 524288 | tf_op jit(solution)/shard_map/all_to_all | solution.py:185
  209.5 0.7 copy.36
  (58 shorter events, 1.8 us)
Async XLA Ops:
  7.2 39.1 %copy-start = (bf16[64,512]{1,0:T(8,128)(2,1)S(1)}, bf16[64,512]{1,0:T(8,128)(2,1)}, u32[]{:S(2)}) copy-start(bf16[64,512]{1,0:T(8,128)(2,1)} %param.18) | copy-start | bytes 196612
  7.2 115.3 %all-gather.2.cloned.1.call-start = ((), (), s32[]{:S(2)}) async-start(), calls=%async_computation.4 | async-start | bytes 8650752 | tf_op jit(solution)/shard_map/all_gather | solution.py:42
  7.9 6.4 %copy-start.9 = (s32[256,1]{0,1:T(1,128)S(1)}, s32[256,1]{0,1:T(1,128)}, u32[]{:S(2)}) copy-start(s32[256,1]{0,1:T(1,128)} %param.14) | copy-start | bytes 3076
  7.9 17.7 %copy-start.5 = (f32[8192]{0:T(1024)S(1)}, f32[8192]{0:T(1024)}, u32[]{:S(2)}) copy-start(f32[8192]{0:T(1024)} %param.16) | copy-start | bytes 98308
  11.1 10.6 %collective-permute-start = (bf16[128,8192]{1,0:T(8,128)(2,1)}, bf16[128,8192]{1,0:T(8,128)(2,1)S(1)}, u32[]{:S(2)}, u32[]{:S(2)}) collective-permute-start(bf16[128,8192]{1,0:T(8,128)(2,1)} %dynamic-slice_bitcast_fusion), channel_id=1, source_target_pairs={{0,128},{128,0},{1,129},{129,1},{2,130},{130,2},{3,131},{131,3},{4... | collective-permute-start | bytes 6291464 | tf_op jit(solution)/shard_map/rows_swap/ppermute | solution.py:52
  15.1 23.1 %all-to-all-start.1 = ((f32[16,1,16]{2,1,0:T(1,128)}), f32[16,1,16]{2,1,0:T(1,128)S(1)}, u32[]{:S(2)}, u32[]{:S(2)}) async-start(f32[16,1,16]{2,1,0:T(1,128)} %broadcast_in_dim.46), calls=%async_computation.1 | async-start | bytes 16384 | tf_op jit(solution)/shard_map/counts/all_to_all | solution.py:93
  21.7 4.0 %copy-start.1 = (bf16[1,256,8192]{2,1,0:T(8,128)(2,1)S(1)}, bf16[1,256,8192]{2,1,0:T(8,128)(2,1)}, u32[]{:S(2)}) copy-start(bf16[1,256,8192]{2,1,0:T(8,128)(2,1)} %param.10) | copy-start | bytes 12582916
  21.7 3.9 %copy-start.2 = (bf16[128,8192]{1,0:T(8,128)(2,1)}, bf16[128,8192]{1,0:T(8,128)(2,1)S(1)}, u32[]{:S(2)}) copy-start(bf16[128,8192]{1,0:T(8,128)(2,1)S(1)} %collective-permute-done) | copy-start | bytes 6291460
  38.1 7.1 %copy-start.4 = (s32[1,256,32]{1,2,0:T(8,128)S(1)}, s32[1,256,32]{1,2,0:T(8,128)}, u32[]{:S(2)}) copy-start(s32[1,256,32]{1,2,0:T(8,128)} %param.13) | copy-start | bytes 98308
  38.1 7.2 %copy-start.7 = (s32[1,256]{1,0:T(1,128)S(1)}, s32[1,256]{1,0:T(1,128)}, u32[]{:S(2)}) copy-start(s32[1,256]{1,0:T(1,128)} %param.12) | copy-start | bytes 3076
  38.1 8.1 %copy-start.8 = (f32[64]{0:T(128)S(1)}, f32[64]{0:T(128)}, u32[]{:S(2)}) copy-start(f32[64]{0:T(128)} %param.15) | copy-start | bytes 772
  38.1 8.4 %copy-start.10 = (bf16[256]{0:T(256)(128)(2,1)S(1)}, bf16[256]{0:T(256)(128)(2,1)}, u32[]{:S(2)}) copy-start(bf16[256]{0:T(256)(128)(2,1)} %param.11) | copy-start | bytes 1540
  38.2 8.9 %copy-start.6 = (bf16[18,512]{1,0:T(8,128)(2,1)S(1)}, bf16[18,512]{1,0:T(8,128)(2,1)}, u32[]{:S(2)}) copy-start(bf16[18,512]{1,0:T(8,128)(2,1)} %param.19) | copy-start | bytes 55300
  38.2 92.1 %all-to-all-start = ((bf16[16,128,512]{1,2,0:T(8,128)(2,1)}), bf16[16,128,512]{1,2,0:T(8,128)(2,1)}, u32[]{:S(2)}, u32[]{:S(2)}) async-start(bf16[16,128,512]{1,2,0:T(8,128)(2,1)} %bitcast.69), calls=%async_computation | async-start | bytes 4194304 | tf_op jit(solution)/shard_map/columns_exchange/all_to_all | solution.py:85
  45.3 1.7 collective-permute-start.1
  128.8 0.8 copy-start.11
  131.0 18.3 %all-to-all-start.2 = ((f32[8,32,256]{2,1,0:T(8,128)}), f32[8,32,256]{2,1,0:T(8,128)S(1)}, u32[]{:S(2)}, u32[]{:S(2)}) async-start(f32[8,32,256]{2,1,0:T(8,128)} %broadcast_in_dim.53), calls=%async_computation.2 | async-start | bytes 524288 | tf_op jit(solution)/shard_map/quant_sum/all_to_all | solution.py:132
  151.0 5.8 %collective-permute-start.2 = (bf16[128,512]{1,0:T(8,128)(2,1)S(1)}, bf16[128,512]{1,0:T(8,128)(2,1)S(1)}, u32[]{:S(2)}, u32[]{:S(2)}) collective-permute-start(bf16[128,512]{1,0:T(8,128)(2,1)S(1)} %fusion.16), channel_id=1, source_target_pairs={{0,24},{8,0},{16,8},{24,16},{32,56},{40,32},{48,40},{56,48},{64,88... | collective-permute-start | bytes 393224 | tf_op jit(solution)/shard_map/grad_gather/ppermute | solution.py:161
  152.7 8.8 %collective-permute-start.3 = (bf16[128,512]{1,0:T(8,128)(2,1)S(1)}, bf16[128,512]{1,0:T(8,128)(2,1)S(1)}, u32[]{:S(2)}, u32[]{:S(2)}) collective-permute-start(bf16[128,512]{1,0:T(8,128)(2,1)S(1)} %fusion.16), channel_id=1, source_target_pairs={{0,16},{8,24},{16,0},{24,8},{32,48},{40,56},{48,32},{56,40},{64,80... | collective-permute-start | bytes 393224 | tf_op jit(solution)/shard_map/grad_gather/ppermute | solution.py:161
  155.0 7.9 %collective-permute-start.4 = (bf16[128,512]{1,0:T(8,128)(2,1)S(1)}, bf16[128,512]{1,0:T(8,128)(2,1)S(1)}, u32[]{:S(2)}, u32[]{:S(2)}) collective-permute-start(bf16[128,512]{1,0:T(8,128)(2,1)S(1)} %fusion.16), channel_id=1, source_target_pairs={{0,8},{8,16},{16,24},{24,0},{32,40},{40,48},{48,56},{56,32},{64,72... | collective-permute-start | bytes 393224 | tf_op jit(solution)/shard_map/grad_gather/ppermute | solution.py:161
  163.0 19.3 %collective-permute-start.5 = (bf16[4,128,512]{2,1,0:T(8,128)(2,1)S(1)}, bf16[4,128,512]{2,1,0:T(8,128)(2,1)S(1)}, u32[]{:S(2)}, u32[]{:S(2)}) collective-permute-start(bf16[4,128,512]{2,1,0:T(8,128)(2,1)S(1)} %pad_maximum_fusion), channel_id=1, source_target_pairs={{0,96},{8,104},{16,112},{24,120},{32,0},{40,8},{48,16},{56,24},{64... | collective-permute-start | bytes 1572872 | tf_op jit(solution)/shard_map/grad_gather/ppermute | solution.py:163
  169.2 13.0 %collective-permute-start.6 = (bf16[4,128,512]{2,1,0:T(8,128)(2,1)S(1)}, bf16[4,128,512]{2,1,0:T(8,128)(2,1)S(1)}, u32[]{:S(2)}, u32[]{:S(2)}) collective-permute-start(bf16[4,128,512]{2,1,0:T(8,128)(2,1)S(1)} %pad_maximum_fusion), channel_id=1, source_target_pairs={{0,32},{8,40},{16,48},{24,56},{32,64},{40,72},{48,80},{56,88},{64,... | collective-permute-start | bytes 1572872 | tf_op jit(solution)/shard_map/grad_gather/ppermute | solution.py:164
  182.2 6.5 %collective-permute-start.7 = (bf16[2,128,512]{2,1,0:T(8,128)(2,1)S(1)}, bf16[2,128,512]{2,1,0:T(8,128)(2,1)S(1)}, u32[]{:S(2)}, u32[]{:S(2)}) collective-permute-start(bf16[2,128,512]{2,1,0:T(8,128)(2,1)S(1)} %slice.76), channel_id=1, source_target_pairs={{0,32},{8,40},{16,48},{24,56},{32,64},{40,72},{48,80},{56,88},{64,... | collective-permute-start | bytes 786440 | tf_op jit(solution)/shard_map/grad_gather/ppermute | solution.py:165
  182.3 6.7 %collective-permute-start.8 = (bf16[2,128,512]{2,1,0:T(8,128)(2,1)S(1)}, bf16[2,128,512]{2,1,0:T(8,128)(2,1)S(1)}, u32[]{:S(2)}, u32[]{:S(2)}) collective-permute-start(bf16[2,128,512]{2,1,0:T(8,128)(2,1)S(1)} %slice.78), channel_id=1, source_target_pairs={{0,96},{8,104},{16,112},{24,120},{32,0},{40,8},{48,16},{56,24},{64... | collective-permute-start | bytes 786440 | tf_op jit(solution)/shard_map/grad_gather/ppermute | solution.py:166
  189.4 5.9 %copy-start.3 = (bf16[256,512]{1,0:T(8,128)(2,1)S(1)}, bf16[256,512]{1,0:T(8,128)(2,1)}, u32[]{:S(2)}) copy-start(bf16[256,512]{1,0:T(8,128)(2,1)} %param.17) | copy-start | bytes 786436
  189.9 5.3 %collective-permute-start.9 = (f32[256,512]{1,0:T(8,128)S(1)}, f32[256,512]{1,0:T(8,128)S(1)}, u32[]{:S(2)}, u32[]{:S(2)}) collective-permute-start(f32[256,512]{1,0:T(8,128)S(1)} %slice.80), channel_id=1, source_target_pairs={{0,128},{128,0},{1,129},{129,1},{2,130},{130,2},{3,131},{131,3},{4... | collective-permute-start | bytes 1572872 | tf_op jit(solution)/shard_map/ppermute | solution.py:183
Sparse Core Ops, SparseCore 0:
  9.9 112.5 all-gather.1
where the time goes:
time: 218 us; the launch traced here: 217 us
  waiting for transfers between devices  106 us (49%)
  starting transfers between devices  43.5 us (20%)
  local copies, waits for them, and re-layouts  15.3 us (7%)
  between operations  14.4 us (7%)
  other arithmetic  14 us (6%)
  blocking collectives  13.3 us (6%)
  matrix products  10.6 us (5%)
    all_gather x1, waiting for transfers between devices, shards(): whole = lax.all_gather(torso_weight, ('grp', 'fsdp'), axis=0, tiled=True)  75.1 us
    all_to_all x1, blocking collectives, shards(): lax.all_to_all(updated, 'tp', split_axis=0, concat_axis=1, tiled=True)  13.3 us
    ppermute x1, waiting for transfers between devices, shards(): above = lax.ppermute(quad, 'fsdp', y_from(3))  11.6 us
    all_to_all x1, waiting for transfers between devices, shards(): lax.all_to_all(jnp.broadcast_to(partial_quant[None], (tp_total,) + partia...  7.69 us
    all_to_all x1, starting transfers between devices, shards(): lax.all_to_all(jnp.broadcast_to(partial_quant[None], (tp_total,) + partia...  7.35 us
    all_to_all x1, starting transfers between devices, shards(): columns = lax.all_to_all(pieces, 'fsdp', 0, 0, tiled=True)  7.1 us
    all_to_all x1, starting transfers between devices, shards(): lax.all_to_all(jnp.broadcast_to(local_counts[None, :], (shard_total, shar...  6.62 us
    dot_general x1, matrix products, shards(): preact = jnp.dot(normed, whole, preferred_element_type=jnp.float32)  6.33 us
  transfers between devices with their start and end apart: 14, of which 8 were waited for; matrix products, arithmetic and copies ran while one was open for 16% of the time, Pallas kernels for 0%

commit v1 on v0

--- a/solution.py
+++ b/solution.py
@@ -39,7 +39,15 @@
     group = lax.axis_index("grp")
     place = lax.axis_index("fsdp")
     shard_total = lax.axis_size("fsdp")
-    whole = lax.all_gather(torso_weight, ("grp", "fsdp"), axis=0, tiled=True)
+    whole = jnp.concatenate(
+        jax.lax.all_to_all(
+            jnp.stack([torso_weight] * jax.lax.axis_size(("grp", "fsdp")), axis=0),
+            ("grp", "fsdp"),
+            0,
+            0,
+        ),
+        axis=0,
+    )
     rows_block = frames.shape[1]
     width = frames.shape[2]
     half = rows_block // 2

time: 218 us -> 347 us (1.59)
  waiting for transfers between devices: 106 us -> 232 us
  blocking collectives: 13.3 us -> 29 us
  between operations: 14.4 us -> 0.97 us
  starting transfers between devices: 43.5 us -> 35.7 us
  local copies, waits for them, and re-layouts: 15.3 us -> 19.7 us
    all_to_all x1, waiting for transfers between devices: 0.01 us -> 155 us  [shards(): jax.lax.all_to_all(jnp.stack([torso_weight] * jax.lax.axis_size(('grp', '...]
    all_gather x1 -> x0, waiting for transfers between devices: 75.1 us -> none  [shards(): whole = lax.all_gather(torso_weight, ('grp', 'fsdp'), axis=0, tiled=True)]
    all_to_all x1, waiting for transfers between devices: 0.01 us -> 39.7 us  [shards(): columns = lax.all_to_all(pieces, 'fsdp', 0, 0, tiled=True)]
    all_to_all x0 -> x1, blocking collectives: none -> 15.7 us  [shards(): lax.all_to_all(jnp.broadcast_to(local_counts[None, :], (shard_total, shar...]
    another operation x0 -> x1, local copies, waits for them, and re-layouts: none -> 5.12 us  [shards(): jnp.stack([torso_weight] * jax.lax.axis_size(('grp', 'fsdp')), axis=0)]
    ppermute x1, starting transfers between devices: 6.18 us -> 2.01 us  [shards(): below = lax.ppermute(quad, 'fsdp', y_from(1))]
    ppermute x2, waiting for transfers between devices: 0.42 us -> 4.47 us  [swap(): got = lax.ppermute(sent, 'grp', SWAP)]
    ppermute x3, waiting for transfers between devices: 6.15 us -> 9.76 us  [shards(): lax.ppermute(grad_preact, 'fsdp', z_from(k))]
  transfers between devices with their start and end apart: 14 -> 13, of which waited for: 8 -> 10; matrix products, arithmetic and copies ran while one was open for 16% -> 10% of each run, Pallas kernels for 0% -> 0%
where the time goes in v1:
time: 347 us; the launch traced here: 343 us
  waiting for transfers between devices  232 us (67%)
  starting transfers between devices  35.7 us (10%)
  blocking collectives  29 us (8%)
  local copies, waits for them, and re-layouts  19.7 us (6%)
  other arithmetic  14.6 us (4%)
  matrix products  10.5 us (3%)
    all_to_all x1, waiting for transfers between devices, shards(): jax.lax.all_to_all(jnp.stack([torso_weight] * jax.lax.axis_size(('grp', '...  155 us
    all_to_all x1, waiting for transfers between devices, shards(): columns = lax.all_to_all(pieces, 'fsdp', 0, 0, tiled=True)  39.7 us
    all_to_all x1, blocking collectives, shards(): lax.all_to_all(jnp.broadcast_to(local_counts[None, :], (shard_total, shar...  15.7 us
    all_to_all x1, blocking collectives, shards(): lax.all_to_all(updated, 'tp', split_axis=0, concat_axis=1, tiled=True)  13.3 us
    ppermute x1, waiting for transfers between devices, shards(): above = lax.ppermute(quad, 'fsdp', y_from(3))  11.9 us
    ppermute x3, waiting for transfers between devices, shards(): lax.ppermute(grad_preact, 'fsdp', z_from(k))  9.76 us
    all_to_all x1, starting transfers between devices, shards(): columns = lax.all_to_all(pieces, 'fsdp', 0, 0, tiled=True)  9.17 us
    all_to_all x1, starting transfers between devices, shards(): lax.all_to_all(jnp.broadcast_to(partial_quant[None], (tp_total,) + partia...  7.95 us
  transfers between devices with their start and end apart: 13, of which 10 were waited for; matrix products, arithmetic and copies ran while one was open for 10% of the time, Pallas kernels for 0%

profile of v1, /device:TPU:1, one launch (start us, length us, event | category | flops | bytes accessed | tf_op | source)
XLA Modules:
  0.0 342.6 jit_solution(107661394960980104)
XLA Ops:
  0.6 0.8 convert_reduce_fusion
  1.5 15.7 %all_to_all.40 = f32[16,1,16]{2,1,0:T(1,128)S(1)} all-to-all(f32[16,1,16]{2,1,0:T(1,128)S(1)} %broadcast_in_dim.46), channel_id=1, replica_groups=mesh['grp'=2,'fsdp'=16,'tp'=8] {'fsdp'}, dimensions={0} | all-to-all | bytes 2048 | tf_op jit(solution)/shard_map/counts/all_to_all | solution.py:101
  17.2 5.1 %stack.15 = bf16[32,256,512]{2,1,0:T(8,128)(2,1)} broadcast(bf16[256,512]{1,0:T(8,128)(2,1)} %param.17), dimensions={1,2} | broadcast | bytes 8650752 | tf_op jit(solution)/shard_map/stack | solution.py:44
  22.3 6.8 %all-to-all-start.2 = ((bf16[32,256,512]{2,1,0:T(8,128)(2,1)}), bf16[32,256,512]{2,1,0:T(8,128)(2,1)}, u32[]{:S(2)}, u32[]{:S(2)}) async-start(bf16[32,256,512]{2,1,0:T(8,128)(2,1)} %stack.15), calls=%async_computation.2 | async-start | bytes 16777216 | tf_op jit(solution)/shard_map/all_to_all | solution.py:43
  29.1 3.1 dynamic-slice_bitcast_fusion
  32.2 0.3 collective-permute-start
  32.5 4.0 %collective-permute-done = bf16[128,8192]{1,0:T(8,128)(2,1)S(1)} collective-permute-done((bf16[128,8192]{1,0:T(8,128)(2,1)}, bf16[128,8192]{1,0:T(8,128)(2,1)S(1)}, u32[]{:S(2)}, u32[]{:S(2)}) %collective-permute-start) | collective-permute-done | bytes 2097184 | tf_op jit(solution)/shard_map/rows_swap/ppermute | solution.py:60
  36.6 3.9 %fusion.3 = (f32[128]{0:T(128)S(1)}, f32[128]{0:T(128)S(1)}) fusion(bf16[128,8192]{1,0:T(8,128)(2,1)S(1)} %collective-permute-done, bf16[1,256,8192]{2,1,0:T(8,128)(2,1)} %param.10, s32[]{:T(128)S(6)} %select_n.75, pred[]{:T(512)S(6)} %eq.32), kind=kLoop, calls=%fused_computation.7 | loop fusion | flops 8388352 | bytes 4195333 | tf_op jit(solution)/shard_map/reduce_sum | solution.py:73
  40.5 4.4 %fusion.5 = (bf16[128,8192]{1,0:T(8,128)(2,1)}, bf16[128,8192]{1,0:T(8,128)(2,1)S(1)}) fusion(f32[128]{0:T(128)S(1)} %get-tuple-element.19, f32[8192]{0:T(1024)S(1)} %copy-done.5, bf16[128,8192]{1,0:T(8,128)(2,1)} %copy-done.2, bf16[1,256,8192]{2,1,0:T(8,128)(2,1)S(1)} %copy-done.1, s32[]{:T(128)S(6)} %select_n.75, pred[]{:T(512)S(6)} %eq.32, ...), kind=kLoop, calls=%fused_computation.9 | loop fusion | flops 10485760 | bytes 8422405 | tf_op jit(solution)/shard_map/convert_element_type | solution.py:74
  44.9 1.2 constant_dynamic-slice_fusion.1
  46.1 2.3 copy.29
  48.3 1.3 copy.30
  49.6 1.7 maximum_bitcast_fusion
  51.4 1.4 copy.31
  52.8 155.1 %all-to-all-done.2 = bf16[32,256,512]{2,1,0:T(8,128)(2,1)} async-done(((bf16[32,256,512]{2,1,0:T(8,128)(2,1)}), bf16[32,256,512]{2,1,0:T(8,128)(2,1)}, u32[]{:S(2)}, u32[]{:S(2)}) %all-to-all-start.2) | async-done | bytes 8388640 | tf_op jit(solution)/shard_map/all_to_all | solution.py:43
  208.0 9.2 %all-to-all-start = ((bf16[16,128,512]{1,2,0:T(8,128)(2,1)}), bf16[16,128,512]{1,2,0:T(8,128)(2,1)}, u32[]{:S(2)}, u32[]{:S(2)}) async-start(bf16[16,128,512]{1,2,0:T(8,128)(2,1)} %bitcast.70), calls=%async_computation | async-start | bytes 4194304 | tf_op jit(solution)/shard_map/columns_exchange/all_to_all | solution.py:93
  217.2 1.2 collective-permute-start.1
  218.3 0.3 fusion.17
  218.7 0.4 collective-permute-done.1
  219.5 6.3 %fusion.6 = f32[256,512]{1,0:T(8,128)S(1)} fusion(bf16[8192,512]{1,0:T(8,128)(2,1)} %bitcast.15, bf16[128,8192]{1,0:T(8,128)(2,1)S(1)} %get-tuple-element.7, bf16[128,8192]{1,0:T(8,128)(2,1)} %get-tuple-element.6), kind=kOutput, calls=%fused_computation.14 | convolution fusion | flops 2155872256 | bytes 13107200 | tf_op jit(solution)/shard_map/dot_general | solution.py:128
  225.8 0.8 copy-done.11
  226.9 0.4 select_reduce_fusion
  227.3 39.7 %all-to-all-done = bf16[16,128,512]{1,2,0:T(8,128)(2,1)} async-done(((bf16[16,128,512]{1,2,0:T(8,128)(2,1)}), bf16[16,128,512]{1,2,0:T(8,128)(2,1)}, u32[]{:S(2)}, u32[]{:S(2)}) %all-to-all-start) | async-done | bytes 2097184 | tf_op jit(solution)/shard_map/columns_exchange/all_to_all | solution.py:93
  267.0 0.7 broadcast_in_dim.53
  267.7 7.9 %all-to-all-start.3 = ((f32[8,32,256]{2,1,0:T(8,128)}), f32[8,32,256]{2,1,0:T(8,128)S(1)}, u32[]{:S(2)}, u32[]{:S(2)}) async-start(f32[8,32,256]{2,1,0:T(8,128)} %broadcast_in_dim.53), calls=%async_computation.3 | async-start | bytes 524288 | tf_op jit(solution)/shard_map/quant_sum/all_to_all | solution.py:140
  276.1 2.8 copy.32
  278.9 6.8 %all-to-all-done.3 = f32[8,32,256]{2,1,0:T(8,128)S(1)} async-done(((f32[8,32,256]{2,1,0:T(8,128)}), f32[8,32,256]{2,1,0:T(8,128)S(1)}, u32[]{:S(2)}, u32[]{:S(2)}) %all-to-all-start.3) | async-done | bytes 262176 | tf_op jit(solution)/shard_map/quant_sum/all_to_all | solution.py:140
  286.1 1.3 fusion.16
  287.4 1.2 collective-permute-start.2
  288.6 0.4 collective-permute-start.4
  289.0 0.7 fusion.11
  289.7 1.6 collective-permute-done.2
  291.3 8.2 %collective-permute-done.3 = bf16[128,512]{1,0:T(8,128)(2,1)S(1)} collective-permute-done((bf16[128,512]{1,0:T(8,128)(2,1)S(1)}, bf16[128,512]{1,0:T(8,128)(2,1)S(1)}, u32[]{:S(2)}, u32[]{:S(2)}) %collective-permute-start.3) | collective-permute-done | bytes 131104 | tf_op jit(solution)/shard_map/grad_gather/ppermute | solution.py:169
  299.6 2.0 collective-permute-start.5
  301.6 0.7 fusion.10
  302.5 11.9 %collective-permute-done.6 = bf16[4,128,512]{2,1,0:T(8,128)(2,1)S(1)} collective-permute-done((bf16[4,128,512]{2,1,0:T(8,128)(2,1)S(1)}, bf16[4,128,512]{2,1,0:T(8,128)(2,1)S(1)}, u32[]{:S(2)}, u32[]{:S(2)}) %collective-permute-start.6) | collective-permute-done | bytes 524320 | tf_op jit(solution)/shard_map/grad_gather/ppermute | solution.py:172
  314.5 2.7 collective-permute-start.8
  317.3 0.5 fusion.34
  317.7 0.5 convolution_add_fusion.1
  318.2 2.7 collective-permute-done.7
  320.9 0.3 fusion.35
  321.3 0.3 fusion.36
  321.6 0.5 fusion.13
  322.1 4.0 %collective-permute-start.9 = (f32[256,512]{1,0:T(8,128)S(1)}, f32[256,512]{1,0:T(8,128)S(1)}, u32[]{:S(2)}, u32[]{:S(2)}) collective-permute-start(f32[256,512]{1,0:T(8,128)S(1)} %slice.80), channel_id=1, source_target_pairs={{0,128},{128,0},{1,129},{129,1},{2,130},{130,2},{3,131},{131,3},{4... | collective-permute-start | bytes 1572872 | tf_op jit(solution)/shard_map/ppermute | solution.py:191
  326.1 1.5 collective-permute-done.9
  327.6 0.9 subtract_convert_fusion
  328.6 13.3 %all_to_all.41 = bf16[8,32,512]{2,1,0:T(8,128)(2,1)S(1)} all-to-all(bf16[8,32,512]{2,1,0:T(8,128)(2,1)S(1)} %bitcast.82), channel_id=1, replica_groups=mesh['grp'=2,'fsdp'=16,'tp'=8] {'tp'}, dimensions={0} | all-to-all | bytes 524288 | tf_op jit(solution)/shard_map/all_to_all | solution.py:193
  341.9 0.7 copy.36
  (57 shorter events, 2.0 us)
Async XLA Ops:
  0.6 217.7 %copy-start = (bf16[64,512]{1,0:T(8,128)(2,1)S(1)}, bf16[64,512]{1,0:T(8,128)(2,1)}, u32[]{:S(2)}) copy-start(bf16[64,512]{1,0:T(8,128)(2,1)} %param.18) | copy-start | bytes 196612
  22.3 185.6 %all-to-all-start.2 = ((bf16[32,256,512]{2,1,0:T(8,128)(2,1)}), bf16[32,256,512]{2,1,0:T(8,128)(2,1)}, u32[]{:S(2)}, u32[]{:S(2)}) async-start(bf16[32,256,512]{2,1,0:T(8,128)(2,1)} %stack.15), calls=%async_computation.2 | async-start | bytes 16777216 | tf_op jit(solution)/shard_map/all_to_all | solution.py:43
  29.1 11.4 %copy-start.5 = (f32[8192]{0:T(1024)S(1)}, f32[8192]{0:T(1024)}, u32[]{:S(2)}) copy-start(f32[8192]{0:T(1024)} %param.16) | copy-start | bytes 98308
  32.2 4.4 %collective-permute-start = (bf16[128,8192]{1,0:T(8,128)(2,1)}, bf16[128,8192]{1,0:T(8,128)(2,1)S(1)}, u32[]{:S(2)}, u32[]{:S(2)}) collective-permute-start(bf16[128,8192]{1,0:T(8,128)(2,1)} %dynamic-slice_bitcast_fusion), channel_id=1, source_target_pairs={{0,128},{128,0},{1,129},{129,1},{2,130},{130,2},{3,131},{131,3},{4... | collective-permute-start | bytes 6291464 | tf_op jit(solution)/shard_map/rows_swap/ppermute | solution.py:60
  32.5 7.9 %copy-start.1 = (bf16[1,256,8192]{2,1,0:T(8,128)(2,1)S(1)}, bf16[1,256,8192]{2,1,0:T(8,128)(2,1)}, u32[]{:S(2)}) copy-start(bf16[1,256,8192]{2,1,0:T(8,128)(2,1)} %param.10) | copy-start | bytes 12582916
  36.6 3.9 %copy-start.2 = (bf16[128,8192]{1,0:T(8,128)(2,1)}, bf16[128,8192]{1,0:T(8,128)(2,1)S(1)}, u32[]{:S(2)}) copy-start(bf16[128,8192]{1,0:T(8,128)(2,1)S(1)} %collective-permute-done) | copy-start | bytes 6291460
  207.9 9.2 %copy-start.4 = (s32[1,256,32]{1,2,0:T(8,128)S(1)}, s32[1,256,32]{1,2,0:T(8,128)}, u32[]{:S(2)}) copy-start(s32[1,256,32]{1,2,0:T(8,128)} %param.13) | copy-start | bytes 98308
  207.9 9.2 %copy-start.7 = (s32[1,256]{1,0:T(1,128)S(1)}, s32[1,256]{1,0:T(1,128)}, u32[]{:S(2)}) copy-start(s32[1,256]{1,0:T(1,128)} %param.12) | copy-start | bytes 3076
  207.9 10.4 %copy-start.8 = (f32[64]{0:T(128)S(1)}, f32[64]{0:T(128)}, u32[]{:S(2)}) copy-start(f32[64]{0:T(128)} %param.15) | copy-start | bytes 772
  207.9 10.7 %copy-start.10 = (bf16[256]{0:T(256)(128)(2,1)S(1)}, bf16[256]{0:T(256)(128)(2,1)}, u32[]{:S(2)}) copy-start(bf16[256]{0:T(256)(128)(2,1)} %param.11) | copy-start | bytes 1540
  207.9 11.3 %copy-start.6 = (bf16[18,512]{1,0:T(8,128)(2,1)S(1)}, bf16[18,512]{1,0:T(8,128)(2,1)}, u32[]{:S(2)}) copy-start(bf16[18,512]{1,0:T(8,128)(2,1)} %param.19) | copy-start | bytes 55300
  208.0 59.0 %all-to-all-start = ((bf16[16,128,512]{1,2,0:T(8,128)(2,1)}), bf16[16,128,512]{1,2,0:T(8,128)(2,1)}, u32[]{:S(2)}, u32[]{:S(2)}) async-start(bf16[16,128,512]{1,2,0:T(8,128)(2,1)} %bitcast.70), calls=%async_computation | async-start | bytes 4194304 | tf_op jit(solution)/shard_map/columns_exchange/all_to_all | solution.py:93
  217.2 2.0 collective-permute-start.1
  225.8 0.8 copy-start.11
  226.6 49.0 %copy-start.9 = (s32[256,1]{0,1:T(1,128)S(1)}, s32[256,1]{0,1:T(1,128)}, u32[]{:S(2)}) copy-start(s32[256,1]{0,1:T(1,128)} %param.14) | copy-start | bytes 3076
  267.7 18.0 %all-to-all-start.3 = ((f32[8,32,256]{2,1,0:T(8,128)}), f32[8,32,256]{2,1,0:T(8,128)S(1)}, u32[]{:S(2)}, u32[]{:S(2)}) async-start(f32[8,32,256]{2,1,0:T(8,128)} %broadcast_in_dim.53), calls=%async_computation.3 | async-start | bytes 524288 | tf_op jit(solution)/shard_map/quant_sum/all_to_all | solution.py:140
  287.4 3.9 %collective-permute-start.2 = (bf16[128,512]{1,0:T(8,128)(2,1)S(1)}, bf16[128,512]{1,0:T(8,128)(2,1)S(1)}, u32[]{:S(2)}, u32[]{:S(2)}) collective-permute-start(bf16[128,512]{1,0:T(8,128)(2,1)S(1)} %fusion.16), channel_id=1, source_target_pairs={{0,24},{8,0},{16,8},{24,16},{32,56},{40,32},{48,40},{56,48},{64,88... | collective-permute-start | bytes 393224 | tf_op jit(solution)/shard_map/grad_gather/ppermute | solution.py:169
  288.6 10.9 %collective-permute-start.3 = (bf16[128,512]{1,0:T(8,128)(2,1)S(1)}, bf16[128,512]{1,0:T(8,128)(2,1)S(1)}, u32[]{:S(2)}, u32[]{:S(2)}) collective-permute-start(bf16[128,512]{1,0:T(8,128)(2,1)S(1)} %fusion.16), channel_id=1, source_target_pairs={{0,16},{8,24},{16,0},{24,8},{32,48},{40,56},{48,32},{56,40},{64,80... | collective-permute-start | bytes 393224 | tf_op jit(solution)/shard_map/grad_gather/ppermute | solution.py:169
  288.6 10.9 %collective-permute-start.4 = (bf16[128,512]{1,0:T(8,128)(2,1)S(1)}, bf16[128,512]{1,0:T(8,128)(2,1)S(1)}, u32[]{:S(2)}, u32[]{:S(2)}) collective-permute-start(bf16[128,512]{1,0:T(8,128)(2,1)S(1)} %fusion.16), channel_id=1, source_target_pairs={{0,8},{8,16},{16,24},{24,0},{32,40},{40,48},{48,56},{56,32},{64,72... | collective-permute-start | bytes 393224 | tf_op jit(solution)/shard_map/grad_gather/ppermute | solution.py:169
  299.6 14.9 %collective-permute-start.5 = (bf16[4,128,512]{2,1,0:T(8,128)(2,1)S(1)}, bf16[4,128,512]{2,1,0:T(8,128)(2,1)S(1)}, u32[]{:S(2)}, u32[]{:S(2)}) collective-permute-start(bf16[4,128,512]{2,1,0:T(8,128)(2,1)S(1)} %pad_maximum_fusion), channel_id=1, source_target_pairs={{0,96},{8,104},{16,112},{24,120},{32,0},{40,8},{48,16},{56,24},{64... | collective-permute-start | bytes 1572872 | tf_op jit(solution)/shard_map/grad_gather/ppermute | solution.py:171
  301.6 12.8 %collective-permute-start.6 = (bf16[4,128,512]{2,1,0:T(8,128)(2,1)S(1)}, bf16[4,128,512]{2,1,0:T(8,128)(2,1)S(1)}, u32[]{:S(2)}, u32[]{:S(2)}) collective-permute-start(bf16[4,128,512]{2,1,0:T(8,128)(2,1)S(1)} %pad_maximum_fusion), channel_id=1, source_target_pairs={{0,32},{8,40},{16,48},{24,56},{32,64},{40,72},{48,80},{56,88},{64,... | collective-permute-start | bytes 1572872 | tf_op jit(solution)/shard_map/grad_gather/ppermute | solution.py:172
  314.4 6.5 %collective-permute-start.7 = (bf16[2,128,512]{2,1,0:T(8,128)(2,1)S(1)}, bf16[2,128,512]{2,1,0:T(8,128)(2,1)S(1)}, u32[]{:S(2)}, u32[]{:S(2)}) collective-permute-start(bf16[2,128,512]{2,1,0:T(8,128)(2,1)S(1)} %slice.76), channel_id=1, source_target_pairs={{0,32},{8,40},{16,48},{24,56},{32,64},{40,72},{48,80},{56,88},{64,... | collective-permute-start | bytes 786440 | tf_op jit(solution)/shard_map/grad_gather/ppermute | solution.py:173
  314.5 6.7 %collective-permute-start.8 = (bf16[2,128,512]{2,1,0:T(8,128)(2,1)S(1)}, bf16[2,128,512]{2,1,0:T(8,128)(2,1)S(1)}, u32[]{:S(2)}, u32[]{:S(2)}) collective-permute-start(bf16[2,128,512]{2,1,0:T(8,128)(2,1)S(1)} %slice.78), channel_id=1, source_target_pairs={{0,96},{8,104},{16,112},{24,120},{32,0},{40,8},{48,16},{56,24},{64... | collective-permute-start | bytes 786440 | tf_op jit(solution)/shard_map/grad_gather/ppermute | solution.py:174
  321.6 6.1 %copy-start.3 = (bf16[256,512]{1,0:T(8,128)(2,1)S(1)}, bf16[256,512]{1,0:T(8,128)(2,1)}, u32[]{:S(2)}) copy-start(bf16[256,512]{1,0:T(8,128)(2,1)} %param.17) | copy-start | bytes 786436
  322.1 5.5 %collective-permute-start.9 = (f32[256,512]{1,0:T(8,128)S(1)}, f32[256,512]{1,0:T(8,128)S(1)}, u32[]{:S(2)}, u32[]{:S(2)}) collective-permute-start(f32[256,512]{1,0:T(8,128)S(1)} %slice.80), channel_id=1, source_target_pairs={{0,128},{128,0},{1,129},{129,1},{2,130},{130,2},{3,131},{131,3},{4... | collective-permute-start | bytes 1572872 | tf_op jit(solution)/shard_map/ppermute | solution.py:191
